TPU v7x, 32 devices: a whole 2x2x4 slice. The times are simulated.
32 devices in a mesh: rows: 16 (over z, y, x), rep: 2 (over core).
Axes of the slice: x: 2, y: 2, z: 4, core: 2. Of those that a mesh axis runs over, the one named last changes fastest.
Arguments:
- features: bfloat16 [4096, 128], P('rows'), may hold values from -6 to 6
- node_order: int32 [4096], P('rows'), may hold values from 0 to 4095, as said below
- tile_vals: bfloat16 [6144, 128, 128], P(('rows', 'rep')), may hold values from -0.0546875 to 0.0546875
- tile_row: int32 [6144], P(('rows', 'rep')), may hold values from 0 to 31, as said below
- tile_col: int32 [6144], P(('rows', 'rep')), may hold values from 0 to 31, as said below
- tile_count: int32 [32], P(('rows', 'rep')), may hold values from 48 to 192, as said below
- weight: bfloat16 [128, 256], replicated, may hold values from -0.5 to 0.5
- bias: float32 [256], replicated, may hold values from -3 to 3
- cotangent: bfloat16 [4096, 256], P('rows'), may hold values from -6 to 6
Outputs:
- activations: bfloat16 [4096, 256], P('rows')
- weight_grad: float32 [128, 256], replicated
- bias_grad: float32 [256], replicated
Inputs may be any that keep to these rules, and one draw needn't show every extreme that they name: `node_order`: positions c * 256 to c * 256 + 255 hold each of the node numbers c * 256 to c * 256 + 255 once. `tile_row`: slots d * 192 to d * 192 + 191 belong to device d = i * 2 + j (i along rows, j along rep); each of them names a row-block from i * 2 to i * 2 + 1. `tile_col`: A slot of device d = i * 2 + j names a column-block c * 2 + j + e for any node group c and any e from 0 to 0; slots may repeat a pair of row-block and column-block. Only the first tile_count[d] slots of device d are live; some device has exactly 192 and some other exactly 48.
All inputs are finite; a program needn't handle non-finite values.
Results may differ from a plain program's by a relative error of at most 0.0056.
Values may be sent and summed in bfloat16 or wider, within the bound.
A program may use at most 128 MiB of HBM per device.

v0:
```python
import jax
import jax.numpy as jnp
from jax import lax
from jax.sharding import PartitionSpec as P


def silu_slope(pre_act):
    sigma = jax.nn.sigmoid(pre_act)
    return sigma * (1.0 + pre_act * (1.0 - sigma))


def body(features, node_order, tile_vals, tile_row, tile_col, tile_count, weight, bias, cotangent):
    row_index = lax.axis_index("rows")
    replica = lax.axis_index("rep")
    replicas = lax.axis_size("rep")
    nodes_dev = features.shape[0]
    feat_width = features.shape[1]
    tile_size = tile_vals.shape[1]
    slot_count = tile_vals.shape[0]
    row_blocks = nodes_dev // tile_size
    half_blocks = row_blocks // replicas
    local_order = node_order - row_index * nodes_dev
    reordered = features[local_order]
    own_half = lax.dynamic_slice_in_dim(
        reordered, replica * half_blocks * tile_size, half_blocks * tile_size, 0
    )
    gathered = lax.all_gather(own_half, "rows", axis=0, tiled=True)
    sources = gathered.reshape(-1, tile_size, feat_width)
    position = tile_col // row_blocks * half_blocks + tile_col % row_blocks - replica * half_blocks
    picked = sources[position]
    products = jnp.einsum("tij,tjf->tif", tile_vals, picked, preferred_element_type=jnp.float32)
    local_rows = tile_row - row_index * row_blocks
    live_mask = (jnp.arange(slot_count, dtype=jnp.int32) < tile_count[0]).astype(jnp.float32)
    select = (local_rows[:, None] == jnp.arange(row_blocks, dtype=jnp.int32)[None, :]).astype(
        jnp.float32
    )
    select = select * live_mask[:, None]
    partial_value = jnp.einsum("tk,tif->kif", select, products, precision=lax.Precision.HIGHEST)
    partial_value = partial_value.reshape(nodes_dev, feat_width)
    grad_reordered = cotangent[local_order]
    grad_scale = float(nodes_dev * lax.axis_size("rows")) ** (-0.5)
    full_total = lax.psum(partial_value, "rep")
    hidden = full_total.astype(jnp.bfloat16)
    pre_act = jnp.dot(hidden, weight, preferred_element_type=jnp.float32) + bias
    activated = jax.nn.silu(pre_act).astype(jnp.bfloat16)
    scaled = (grad_reordered.astype(jnp.float32) * silu_slope(pre_act)).astype(jnp.bfloat16)
    weight_term = lax.dot_general(
        hidden, scaled, (((0,), (0,)), ((), ())), preferred_element_type=jnp.float32
    )
    bias_term = jnp.sum(scaled.astype(jnp.float32), axis=0)
    weight_grad, bias_grad = lax.psum((weight_term, bias_term), "rows")
    activations = jnp.zeros_like(activated).at[local_order].set(activated)
    return (activations, weight_grad * grad_scale, bias_grad * grad_scale)


def solution(mesh):
    return jax.shard_map(
        body,
        mesh=mesh,
        in_specs=(
            P("rows", None),
            P("rows"),
            P(("rows", "rep"), None, None),
            P(("rows", "rep")),
            P(("rows", "rep")),
            P(("rows", "rep")),
            P(),
            P(),
            P("rows", None),
        ),
        out_specs=(P("rows", None), P(), P()),
        check_vma=False,
    )
```

profile of v0, /device:TPU:0, one launch (start us, length us, event | category | flops | bytes accessed | tf_op | source)
XLA Modules:
  0.0 216.0 jit_solution(16689226755002568586)
XLA Ops:
  7.2 0.0 copy-start
  7.2 0.0 all-reduce.3.cloned.1.call-start
  7.2 0.7 compare_select_fusion.2
  7.9 1.6 gather_fusion
  9.5 45.3 %all_gather.3 = bf16[2048,128]{1,0:T(8,128)(2,1)S(1)} all-gather(bf16[128,128]{1,0:T(8,128)(2,1)S(1)} %constant_dynamic-slice_fusion), channel_id=1, replica_groups=mesh['rows'=16,'rep'=2] {'rows'}, dimensions={0}, use_global_device_ids=true | all-gather | bytes 557056 | tf_op jit(solution)/shard_map/all_gather | solution.py:27
  54.8 0.7 compare_select_fusion
  55.5 8.0 %gather_fusion.1 = bf16[192,128,128]{2,1,0:T(8,128)(2,1)} fusion(bf16[16,128,128]{2,1,0:T(8,128)(2,1)S(1)} %bitcast.16, s32[1024]{0:T(1024)S(1)} %pad_clamp_fusion), kind=kCustom, calls=%fused_computation.1 | custom fusion | bytes 12583680 | tf_op jit(solution)/shard_map/gather | solution.py:30
  63.5 13.7 %fusion.15 = f32[192,128,128]{2,1,0:T(8,128)} fusion(bf16[192,128,128]{2,1,0:T(8,128)(2,1)} %gather_fusion.1, bf16[192,128,128]{2,1,0:T(8,128)(2,1)} %param.11), kind=kOutput, calls=%fused_computation.38 | convolution fusion | flops 805306368 | bytes 25165824 | tf_op jit(solution)/shard_map/tij,tjf->tif/dot_general | solution.py:31
  77.2 0.0 copy-start.1
  77.2 12.7 %copy.13 = f32[192,128,128]{1,0,2:T(8,128)} copy(f32[192,128,128]{2,1,0:T(8,128)} %fusion.15) | data formatting | bytes 25165824 | tf_op jit(solution)/shard_map/tij,tjf->tif/dot_general | solution.py:31
  90.6 0.0 copy-done.1
  90.6 0.0 copy-start.2
  90.6 0.0 copy-start.3
  90.6 8.9 %fusion = f32[2,128,128]{2,0,1:T(2,128)S(1)} fusion(f32[192,128,128]{1,0,2:T(8,128)} %copy.13, f32[192]{0:T(256)S(1)} %compare_convert_fusion, s32[192]{0:T(256)S(1)} %broadcast_subtract_fusion), kind=kOutput, calls=%fused_computation.4 | convolution fusion | flops 75498240 | bytes 12715520 | tf_op jit(solution)/shard_map/tk,tif->kif/dot_general | solution.py:38
  99.6 3.8 %all-reduce.4 = bf16[256,128]{1,0:T(8,128)(2,1)S(1)} all-reduce(f32[256,128]{1,0:T(8,128)S(1)} %bitcast.17), channel_id=1, replica_groups=mesh['rows'=16,'rep'=2] {'rep'}, use_global_device_ids=true, to_apply=%region_0.1 | all-reduce | flops 32768 | bytes 196608 | tf_op jit(solution)/shard_map/psum | solution.py:42
  103.4 0.0 copy-done
  103.4 1.2 gather_fusion.2
  104.6 0.0 copy-done.2
  104.6 0.0 copy-done.3
  104.6 0.3 convert_reduce_fusion
  104.9 0.9 fusion.16
  105.7 0.0 all-reduce.3.cloned.1.call-update
  105.8 36.6 %psum.23 = f32[256]{0:T(256)S(1)} all-reduce(f32[256]{0:T(256)S(1)} %get-tuple-element.3), channel_id=1, replica_groups=mesh['rows'=16,'rep'=2] {'rows'}, use_global_device_ids=true, to_apply=%region_4.5 | all-reduce | flops 256 | bytes 2048 | tf_op jit(solution)/shard_map/psum | solution.py:51
  142.4 2.1 scatter_custom_fusion
  144.5 0.6 broadcast_multiply_fusion.1
  145.1 62.5 %all-reduce.3.cloned.1.call-done = f32[128,256]{1,0:T(8,128)} async-done(((f32[128,256]{1,0:T(8,128)}), f32[128,256]{1,0:T(8,128)}) %all-reduce.3.cloned.1.call-update) | async-done | bytes 131088 | tf_op jit(solution)/shard_map/psum | solution.py:51
  207.6 1.6 broadcast_multiply_fusion
  (6 shorter events, 0.0 us)
Async XLA Ops:
  7.2 96.3 %copy-start = (bf16[256,256]{1,0:T(8,128)(2,1)S(1)}, bf16[256,256]{1,0:T(8,128)(2,1)}, u32[]{:S(2)}) copy-start(bf16[256,256]{1,0:T(8,128)(2,1)} %param.17) | copy-start | bytes 393220
  7.2 200.4 %all-reduce.3.cloned.1.call-start = ((), (), s32[]{:S(2)}) async-start(), calls=%async_computation | async-start | bytes 262144 | tf_op jit(solution)/shard_map/psum | solution.py:51
  77.2 13.4 %copy-start.1 = (s32[192]{0:T(256)S(1)}, s32[192]{0:T(256)}, u32[]{:S(2)}) copy-start(s32[192]{0:T(256)} %param.12) | copy-start | bytes 2308
  90.6 14.0 %copy-start.2 = (bf16[128,256]{1,0:T(8,128)(2,1)S(1)}, bf16[128,256]{1,0:T(8,128)(2,1)}, u32[]{:S(2)}) copy-start(bf16[128,256]{1,0:T(8,128)(2,1)} %param.15) | copy-start | bytes 196612
  90.6 14.0 %copy-start.3 = (f32[256]{0:T(256)S(1)}, f32[256]{0:T(256)}, u32[]{:S(2)}) copy-start(f32[256]{0:T(256)} %param.16) | copy-start | bytes 3076
Sparse Core Ops, SparseCore 0:
  105.9 101.6 all-reduce.2
where the time goes:
time: 216 us
  blocking collectives  85.8 us (40%)
  waiting for transfers between devices  62.5 us (29%)
  matrix products  23.8 us (11%)
  local copies, waits for them, and re-layouts  23.4 us (11%)
  between operations  14.8 us (7%)
  other arithmetic  5.66 us (3%)
    psum x1, waiting for transfers between devices, body(): weight_grad, bias_grad = lax.psum((weight_term, bias_term), 'rows')  62.5 us
    all_gather x1, blocking collectives, body(): gathered = lax.all_gather(own_half, 'rows', axis=0, tiled=True)  45.3 us
    psum x1, blocking collectives, body(): weight_grad, bias_grad = lax.psum((weight_term, bias_term), 'rows')  36.6 us
    dot_general x1, matrix products, body(): jnp.einsum('tij,tjf->tif', tile_vals, picked, preferred_element_type=jnp....  13.7 us
    dot_general x1, local copies, waits for them, and re-layouts, body(): jnp.einsum('tij,tjf->tif', tile_vals, picked, preferred_element_type=jnp....  12.7 us
    dot_general x1, matrix products, body(): jnp.einsum('tk,tif->kif', select, products, precision=lax.Precision.HIGHEST)  8.91 us
    gather x1, local copies, waits for them, and re-layouts, body(): picked = sources[position]  7.99 us
  transfers between devices with their start and end apart: 1, of which 1 were waited for; matrix products, arithmetic and copies ran while one was open for 1% of the time, Pallas kernels for 0%

commit v1 on v0

v1 whole, which is shorter than its diff:
```python
import functools

import jax
import jax.numpy as jnp
from jax import lax
from jax.experimental import pallas as pl
from jax.experimental.pallas import tpu as pltpu
from jax.sharding import PartitionSpec as P

MESH = pl.DeviceIdType.MESH
SUBLANES = 8
CONTRACT_ROWS = (((0,), (0,)), ((), ()))


def kernel(
    n_rows, replicas, reducers, chunks, unroll,
    tile_row, tile_col, tile_count, order, features, weight, bias, cotangent, tiles_hbm,
    act_out, weight_out, bias_out,
    tiles, reordered, sources, grad_reordered, parts, terms, landed, finals,
    tile_sem, gather_send, gather_recv, part_send, part_recv, term_send, term_recv,
    final_send, final_recv,
):
    row = lax.axis_index("rows")
    replica = lax.axis_index("rep")
    slots, tile_size, _ = tiles.shape
    nodes, feat_width = features.shape
    hid = cotangent.shape[1]
    row_blocks = nodes // tile_size
    half_blocks = row_blocks // replicas
    zero_block = n_rows * half_blocks
    slice_rows = feat_width // reducers
    col_width = hid // replicas
    per_chunk = slots // chunks
    devices = n_rows * replicas

    def tile_copy(chunk):
        span = pl.ds(chunk * per_chunk, per_chunk)
        return pltpu.make_async_copy(tiles_hbm.at[span], tiles.at[span], tile_sem.at[chunk])

    for chunk in range(chunks):
        tile_copy(chunk).start()

    barrier = pltpu.get_barrier_semaphore()
    me = row * replicas + replica

    @pl.loop(1, devices)
    def _(off):
        other = lax.rem(me + off, devices)
        pl.semaphore_signal(
            barrier, inc=1, device_id=(other // replicas, lax.rem(other, replicas)),
            device_id_type=MESH,
        )

    local = order[...] - row * nodes
    place = (lax.broadcasted_iota(jnp.int32, (nodes, nodes), 0) == local).astype(jnp.bfloat16)
    mine = lax.dot_general(
        place, features[...], CONTRACT_ROWS, preferred_element_type=jnp.float32
    ).astype(jnp.bfloat16)
    reordered[...] = mine.reshape(row_blocks, tile_size, feat_width)
    sources[zero_block] = jnp.zeros((tile_size, feat_width), jnp.bfloat16)
    own_blocks = pl.ds(replica * half_blocks, half_blocks)
    sources[pl.ds(row * half_blocks, half_blocks)] = reordered[own_blocks]

    pl.semaphore_wait(barrier, devices - 1)

    def gather_copy(source, target):
        return pltpu.make_async_remote_copy(
            src_ref=reordered.at[own_blocks],
            dst_ref=sources.at[pl.ds(source * half_blocks, half_blocks)],
            send_sem=gather_send.at[target],
            recv_sem=gather_recv.at[source],
            device_id=(target, replica),
            device_id_type=MESH,
        )

    @pl.loop(1, n_rows)
    def _(off):
        gather_copy(row, lax.rem(row + off, n_rows)).start()

    grad_reordered[...] = lax.dot_general(
        place, cotangent[...], CONTRACT_ROWS, preferred_element_type=jnp.float32
    )

    for chunk in range(chunks):
        tile_copy(chunk).wait()

    @pl.loop(1, n_rows)
    def _(off):
        gather_copy(lax.rem(row + n_rows - off, n_rows), row).wait_recv()

    live = tile_count[0]
    first_block = row * row_blocks

    def aggregate(step, acc):
        left, right = [], []
        for sub in range(unroll):
            slot = step * unroll + sub
            col = tile_col[slot]
            position = (
                col // row_blocks * half_blocks + lax.rem(col, row_blocks) - replica * half_blocks
            )
            block = jnp.where(slot < live, tile_row[slot] - first_block, row_blocks)
            left.append(tiles[slot])
            right.append(
                jnp.concatenate(
                    [
                        sources[jnp.where(block == which, position, zero_block)]
                        for which in range(row_blocks)
                    ],
                    axis=1,
                )
            )
        return acc + jnp.dot(
            jnp.concatenate(left, axis=1),
            jnp.concatenate(right, axis=0),
            preferred_element_type=jnp.float32,
        )

    acc = lax.fori_loop(
        0, slots // unroll, aggregate, jnp.zeros((tile_size, row_blocks * feat_width), jnp.float32)
    )
    for which in range(row_blocks):
        parts[replica, which] = acc[:, which * feat_width:(which + 1) * feat_width]

    def part_copy(source, target):
        return pltpu.make_async_remote_copy(
            src_ref=parts.at[source],
            dst_ref=parts.at[source],
            send_sem=part_send.at[target],
            recv_sem=part_recv.at[source],
            device_id=(row, target),
            device_id_type=MESH,
        )

    for off in range(1, replicas):
        part_copy(replica, lax.rem(replica + off, replicas)).start()
    for off in range(1, replicas):
        part_copy(lax.rem(replica + replicas - off, replicas), replica).wait_recv()

    total = parts[0]
    for which in range(1, replicas):
        total = total + parts[which]
    hidden = total.reshape(nodes, feat_width).astype(jnp.bfloat16)
    pre_act = jnp.dot(hidden, weight[...], preferred_element_type=jnp.float32) + bias[...]
    sigma = 1.0 / (1.0 + jnp.exp(-pre_act))
    slope = sigma * (1.0 + pre_act * (1.0 - sigma))
    scaled = (grad_reordered[...] * slope).astype(jnp.bfloat16)
    weight_term = lax.dot_general(
        hidden, scaled, CONTRACT_ROWS, preferred_element_type=jnp.float32
    )
    bias_term = jnp.sum(scaled.astype(jnp.float32), axis=0, keepdims=True)
    pad = jnp.zeros((SUBLANES - replicas, col_width), jnp.float32)
    bias_rows = jnp.concatenate(
        [bias_term[:, j * col_width:(j + 1) * col_width] for j in range(replicas)] + [pad], axis=0
    )
    for j in range(replicas):
        terms[j, :, :slice_rows] = weight_term[:, j * col_width:(j + 1) * col_width].reshape(
            reducers, slice_rows, col_width
        )
        for k in range(reducers):
            terms[j, k, slice_rows:] = bias_rows

    def term_copy(source, target):
        return pltpu.make_async_remote_copy(
            src_ref=terms.at[replica, target],
            dst_ref=landed.at[source],
            send_sem=term_send.at[target],
            recv_sem=term_recv.at[source],
            device_id=(target, replica),
            device_id_type=MESH,
        )

    def final_copy(source, source_rep, target, target_rep):
        return pltpu.make_async_remote_copy(
            src_ref=finals.at[source, source_rep],
            dst_ref=finals.at[source, source_rep],
            send_sem=final_send.at[target, target_rep],
            recv_sem=final_recv.at[source, source_rep],
            device_id=(target, target_rep),
            device_id_type=MESH,
        )

    def for_reducers(action):
        @pl.loop(0, reducers)
        def _(k):
            @pl.when(k != row)
            def _():
                action(k)

    for_reducers(lambda k: term_copy(row, k).start())

    activated = (pre_act * sigma).astype(jnp.bfloat16)
    act_out[...] = jnp.dot(place, activated, preferred_element_type=jnp.float32).astype(
        jnp.bfloat16
    )

    def reduce_slice():
        landed[row] = terms[replica, row]

        @pl.loop(1, n_rows)
        def _(off):
            term_copy(lax.rem(row + n_rows - off, n_rows), row).wait_recv()

        summed = landed[0]
        for k in range(1, n_rows):
            summed = summed + landed[k]
        finals[row, replica] = summed * float(nodes * n_rows) ** (-0.5)

        @pl.loop(1, devices)
        def _(off):
            other = lax.rem(me + off, devices)
            final_copy(row, replica, other // replicas, lax.rem(other, replicas)).start()

    if reducers == n_rows:
        reduce_slice()
    else:
        pl.when(row < reducers)(reduce_slice)

    def for_finals(action):
        @pl.loop(0, reducers * replicas)
        def _(k):
            @pl.when(k != me)
            def _():
                action(k // replicas, lax.rem(k, replicas))

    for_finals(lambda k, j: final_copy(k, j, row, replica).wait_recv())
    for j in range(replicas):
        weight_out[:, j * col_width:(j + 1) * col_width] = finals[:, j, :slice_rows].reshape(
            feat_width, col_width
        )
        bias_out[:, j * col_width:(j + 1) * col_width] = finals[0, 0, slice_rows + j:slice_rows + j + 1]

    @pl.loop(1, n_rows)
    def _(off):
        gather_copy(row, lax.rem(row + off, n_rows)).wait_send()

    for off in range(1, replicas):
        part_copy(replica, lax.rem(replica + off, replicas)).wait_send()
    for_reducers(lambda k: term_copy(row, k).wait_send())

    def drain():
        @pl.loop(1, devices)
        def _(off):
            other = lax.rem(me + off, devices)
            final_copy(row, replica, other // replicas, lax.rem(other, replicas)).wait_send()

    if reducers == n_rows:
        drain()
    else:
        pl.when(row < reducers)(drain)


def body(n_rows, replicas, features, node_order, tile_vals, tile_row, tile_col, tile_count, weight, bias, cotangent):
    nodes, feat_width = features.shape
    hid = cotangent.shape[1]
    slots, tile_size, _ = tile_vals.shape
    row_blocks = nodes // tile_size
    half_blocks = row_blocks // replicas
    reducers = min(n_rows, feat_width // SUBLANES)
    slice_rows = feat_width // reducers
    payload = slice_rows + SUBLANES
    col_width = hid // replicas
    chunks = 4
    vmem = pl.BlockSpec(memory_space=pltpu.VMEM)
    smem = pl.BlockSpec(memory_space=pltpu.SMEM)
    dma = pltpu.SemaphoreType.DMA
    activations, weight_grad, bias_grad = pl.pallas_call(
        functools.partial(kernel, n_rows, replicas, reducers, chunks, 8),
        out_shape=(
            jax.ShapeDtypeStruct((nodes, hid), jnp.bfloat16),
            jax.ShapeDtypeStruct((feat_width, hid), jnp.float32),
            jax.ShapeDtypeStruct((1, hid), jnp.float32),
        ),
        in_specs=[smem] * 3 + [vmem] * 5 + [pl.BlockSpec(memory_space=pl.ANY)],
        out_specs=(vmem, vmem, vmem),
        scratch_shapes=[
            pltpu.VMEM((slots, tile_size, tile_size), jnp.bfloat16),
            pltpu.VMEM((row_blocks, tile_size, feat_width), jnp.bfloat16),
            pltpu.VMEM((n_rows * half_blocks + 1, tile_size, feat_width), jnp.bfloat16),
            pltpu.VMEM((nodes, hid), jnp.float32),
            pltpu.VMEM((replicas, row_blocks, tile_size, feat_width), jnp.float32),
            pltpu.VMEM((replicas, reducers, payload, col_width), jnp.float32),
            pltpu.VMEM((n_rows, payload, col_width), jnp.float32),
            pltpu.VMEM((reducers, replicas, payload, col_width), jnp.float32),
            dma((chunks,)),
            dma((n_rows,)),
            dma((n_rows,)),
            dma((replicas,)),
            dma((replicas,)),
            dma((reducers,)),
            dma((n_rows,)),
            dma((n_rows, replicas)),
            dma((reducers, replicas)),
        ],
        compiler_params=pltpu.CompilerParams(
            collective_id=0, has_side_effects=True, vmem_limit_bytes=48 * 1024 * 1024
        ),
    )(
        tile_row, tile_col, tile_count, node_order.reshape(1, nodes), features, weight,
        bias.reshape(1, hid), cotangent, tile_vals,
    )
    return activations, weight_grad, bias_grad.reshape(hid)


def solution(mesh):
    return jax.shard_map(
        functools.partial(body, mesh.shape["rows"], mesh.shape["rep"]),
        mesh=mesh,
        in_specs=(
            P("rows", None),
            P("rows"),
            P(("rows", "rep"), None, None),
            P(("rows", "rep")),
            P(("rows", "rep")),
            P(("rows", "rep")),
            P(),
            P(),
            P("rows", None),
        ),
        out_specs=(P("rows", None), P(), P()),
        check_vma=False,
    )
```

time: 216 us -> 50.5 us (0.23)
  the two profiles are of different devices: /device:TPU:0 before, /device:TPU:15 now
where the time goes in v1:
time: 50.5 us; the launch traced here: 50.2 us
  Pallas kernels  41.8 us (83%)
  local copies, waits for them, and re-layouts  7.16 us (14%)
  between operations  1.3 us (3%)
    pallas_call x1, Pallas kernels, body(): pl.pallas_call(functools.partial(kernel, n_rows, replicas, reducers, chun...  41.8 us
    unnamed x17, local copies, waits for them, and re-layouts  7.16 us

profile of v1, /device:TPU:15, one launch (start us, length us, event | category | flops | bytes accessed | tf_op | source)
XLA Modules:
  0.0 50.2 jit_solution(13274565111303615163)
XLA Ops:
  1.3 0.0 copy-start
  1.3 0.9 %copy-done = bf16[256,256]{1,0:T(8,128)(2,1)S(1)} copy-done((bf16[256,256]{1,0:T(8,128)(2,1)S(1)}, bf16[256,256]{1,0:T(8,128)(2,1)}, u32[]{:S(2)}) %copy-start) | copy-done | bytes 131096
  2.2 0.0 copy-start.1
  2.2 0.8 %copy-done.1 = bf16[256,128]{1,0:T(8,128)(2,1)S(1)} copy-done((bf16[256,128]{1,0:T(8,128)(2,1)S(1)}, bf16[256,128]{1,0:T(8,128)(2,1)}, u32[]{:S(2)}) %copy-start.1) | copy-done | bytes 65560
  3.0 0.0 copy-start.2
  3.0 0.8 %copy-done.2 = bf16[128,256]{1,0:T(8,128)(2,1)S(1)} copy-done((bf16[128,256]{1,0:T(8,128)(2,1)S(1)}, bf16[128,256]{1,0:T(8,128)(2,1)}, u32[]{:S(2)}) %copy-start.2) | copy-done | bytes 65560
  3.9 0.0 copy-start.3
  3.9 0.7 %copy-done.3 = s32[192]{0:T(256)S(1)} copy-done((s32[192]{0:T(256)S(1)}, s32[192]{0:T(256)}, u32[]{:S(2)}) %copy-start.3) | copy-done | bytes 792
  4.5 0.0 copy-start.4
  4.5 0.7 %copy-done.4 = s32[192]{0:T(256)S(1)} copy-done((s32[192]{0:T(256)S(1)}, s32[192]{0:T(256)}, u32[]{:S(2)}) %copy-start.4) | copy-done | bytes 792
  5.2 0.0 copy-start.5
  5.2 0.7 %copy-done.5 = s32[256]{0:T(256)S(1)} copy-done((s32[256]{0:T(256)S(1)}, s32[256]{0:T(256)}, u32[]{:S(2)}) %copy-start.5) | copy-done | bytes 1048
  5.9 0.0 copy-start.6
  5.9 0.7 %copy-done.6 = f32[256]{0:T(256)S(1)} copy-done((f32[256]{0:T(256)S(1)}, f32[256]{0:T(256)}, u32[]{:S(2)}) %copy-start.6) | copy-done | bytes 1048
  6.6 41.8 %shard_map.112 = (bf16[256,256]{1,0:T(8,128)(2,1)S(1)}, f32[128,256]{1,0:T(8,128)S(1)}, f32[1,256]{1,0:T(1,128)S(1)}) custom-call(s32[192]{0:T(256)S(1)} %copy-done.3, s32[192]{0:T(256)S(1)} %copy-done.4, s32[1]{0:T(128)S(6)} %copy.15.tile_count, s32[1,256]{1,0:T(1,128)S(1)} %bitcast.3, bf16[256,128]{1,0:T(8,128)(2,1)S(1)} %copy-done.1, ...), custom_call_target="tpu_custom_call" | custom-call | tf_op jit(solution)/shard_map/pallas_call | solution.py:267
  48.3 0.7 %copy.16 = bf16[256,256]{1,0:T(8,128)(2,1)} copy(bf16[256,256]{1,0:T(8,128)(2,1)S(1)} %get-tuple-element.12) | data formatting | bytes 262144
  49.0 0.7 %copy.17 = f32[128,256]{1,0:T(8,128)} copy(f32[128,256]{1,0:T(8,128)S(1)} %get-tuple-element.13) | data formatting | bytes 262144
  49.7 0.6 %copy.18 = f32[256]{0:T(256)} copy(f32[256]{0:T(256)S(1)} %bitcast.5) | data formatting | bytes 2048
Async XLA Ops:
  1.3 0.9 %copy-start = (bf16[256,256]{1,0:T(8,128)(2,1)S(1)}, bf16[256,256]{1,0:T(8,128)(2,1)}, u32[]{:S(2)}) copy-start(bf16[256,256]{1,0:T(8,128)(2,1)} %cotangent.1) | copy-start | bytes 393220
  2.2 0.8 %copy-start.1 = (bf16[256,128]{1,0:T(8,128)(2,1)S(1)}, bf16[256,128]{1,0:T(8,128)(2,1)}, u32[]{:S(2)}) copy-start(bf16[256,128]{1,0:T(8,128)(2,1)} %features.1) | copy-start | bytes 196612
  3.0 0.8 %copy-start.2 = (bf16[128,256]{1,0:T(8,128)(2,1)S(1)}, bf16[128,256]{1,0:T(8,128)(2,1)}, u32[]{:S(2)}) copy-start(bf16[128,256]{1,0:T(8,128)(2,1)} %weight.1) | copy-start | bytes 196612
  3.9 0.7 %copy-start.3 = (s32[192]{0:T(256)S(1)}, s32[192]{0:T(256)}, u32[]{:S(2)}) copy-start(s32[192]{0:T(256)} %tile_row.1) | copy-start | bytes 2308
  4.5 0.7 %copy-start.4 = (s32[192]{0:T(256)S(1)}, s32[192]{0:T(256)}, u32[]{:S(2)}) copy-start(s32[192]{0:T(256)} %tile_col.1) | copy-start | bytes 2308
  5.2 0.7 %copy-start.5 = (s32[256]{0:T(256)S(1)}, s32[256]{0:T(256)}, u32[]{:S(2)}) copy-start(s32[256]{0:T(256)} %param.10) | copy-start | bytes 3076
  5.9 0.7 %copy-start.6 = (f32[256]{0:T(256)S(1)}, f32[256]{0:T(256)}, u32[]{:S(2)}) copy-start(f32[256]{0:T(256)} %param.16) | copy-start | bytes 3076

commit v2 on v1

v2 whole, which is shorter than its diff:
```python
import functools
import math

import jax
import jax.numpy as jnp
from jax import lax
from jax.experimental import pallas as pl
from jax.experimental.pallas import tpu as pltpu
from jax.sharding import PartitionSpec as P

MESH = pl.DeviceIdType.MESH
BIAS_ROWS = 16
CONTRACT_ROWS = (((0,), (0,)), ((), ()))


def kernel(
    n_rows, replicas, plane, chunks, unroll,
    tile_row_hbm, tile_col_hbm, tile_count_hbm, order_hbm, features_hbm, weight_hbm, bias_hbm,
    cotangent_hbm, tiles_hbm,
    act_out, weight_out, bias_out,
    tile_row, tile_col, tile_count, order, features, weight, bias, cotangent, activated, input_sem,
    act_sem, tiles, sources, grad_reordered, parts, terms, finals,
    tile_sem, gather_column, gather_plane, gather_recv, part_send, part_recv,
    term_column, term_plane, term_recv, final_send, final_recv,
):
    row = lax.axis_index("rows")
    replica = lax.axis_index("rep")
    slots, tile_size, _ = tiles.shape
    nodes, feat_width = features.shape
    hid = cotangent.shape[1]
    row_blocks = nodes // tile_size
    half_blocks = row_blocks // replicas
    zero_block = n_rows * half_blocks
    col_width = hid // replicas
    per_chunk = slots // chunks
    depth = n_rows // plane
    layer = row // plane
    spot = lax.rem(row, plane)
    toward = 1 - 2 * (layer // ((depth + 1) // 2))

    def column_peer(off):
        return lax.rem(layer + toward * off + depth, depth) * plane + spot

    def plane_peer(off):
        return layer * plane + lax.rem(spot + off, plane)

    inputs = [
        pltpu.make_async_copy(source, target, input_sem.at[k])
        for k, (source, target) in enumerate([
            (order_hbm, order), (features_hbm, features), (cotangent_hbm, cotangent),
            (tile_row_hbm, tile_row), (tile_col_hbm, tile_col), (tile_count_hbm, tile_count),
            (weight_hbm, weight), (bias_hbm, bias),
        ])
    ]
    for copy in inputs:
        copy.start()

    def tile_copy(chunk):
        span = pl.ds(chunk * per_chunk, per_chunk)
        return pltpu.make_async_copy(tiles_hbm.at[span], tiles.at[span], tile_sem.at[chunk])

    for chunk in range(chunks):
        tile_copy(chunk).start()

    barrier = pltpu.get_barrier_semaphore()

    def greet(target, target_rep):
        pl.semaphore_signal(
            barrier, inc=1, device_id=(target, target_rep), device_id_type=MESH
        )

    @pl.loop(1, depth)
    def _(off):
        greet(column_peer(off), replica)

    for off in range(1, plane):
        greet(plane_peer(off), replica)
    for off in range(1, replicas):
        greet(row, lax.rem(replica + off, replicas))

    class Spread:
        def __init__(self, view, column_sem, plane_sem, recv_sem):
            self.view, self.recv_sem = view, recv_sem
            self.column_sem, self.plane_sem = column_sem, plane_sem

        def copy(self, block, target, send_sem):
            return pltpu.make_async_remote_copy(
                src_ref=self.view(block),
                dst_ref=self.view(block),
                send_sem=send_sem,
                recv_sem=self.recv_sem.at[block],
                device_id=(target, replica),
                device_id_type=MESH,
            )

        def along_column(self, off):
            return self.copy(row, column_peer(off), self.column_sem.at[off])

        def through_plane(self, step, off):
            block = row if step is None else column_peer(step)
            step = 0 if step is None else step
            return self.copy(block, plane_peer(off), self.plane_sem.at[step, off])

        def start(self):
            @pl.loop(1, depth)
            def _(off):
                self.along_column(depth - off).start()

            for off in range(1, plane):
                self.through_plane(None, off).start()

        def relay(self):
            @pl.loop(1, depth)
            def _(step):
                self.copy(column_peer(step), row, self.column_sem.at[0]).wait_recv()
                for off in range(1, plane):
                    self.through_plane(step, off).start()

        def finish(self):
            for off in range(1, plane):
                beside = lax.rem(spot + off, plane)

                @pl.loop(0, depth)
                def _(level):
                    self.copy(level * plane + beside, row, self.column_sem.at[0]).wait_recv()

        def drain(self):
            @pl.loop(1, depth)
            def _(off):
                self.along_column(off).wait_send()
                for beside in range(1, plane):
                    self.through_plane(off, beside).wait_send()

            for off in range(1, plane):
                self.through_plane(None, off).wait_send()

    def source_view(block):
        return sources.at[pl.ds(block * half_blocks, half_blocks)]

    gather = Spread(source_view, gather_column, gather_plane, gather_recv)
    reduction = Spread(lambda block: terms.at[block], term_column, term_plane, term_recv)

    inputs[0].wait()
    inputs[1].wait()
    local = order[...] - row * nodes
    place = (lax.broadcasted_iota(jnp.int32, (nodes, nodes), 0) == local).astype(jnp.bfloat16)
    mine = lax.dot_general(
        place, features[...], CONTRACT_ROWS, preferred_element_type=jnp.float32
    ).astype(jnp.bfloat16).reshape(replicas, half_blocks, tile_size, feat_width)
    own = mine[0]
    for which in range(1, replicas):
        own = jnp.where(replica == which, mine[which], own)
    sources[pl.ds(row * half_blocks, half_blocks)] = own
    sources[zero_block] = jnp.zeros((tile_size, feat_width), jnp.bfloat16)

    pl.semaphore_wait(barrier, depth - 1 + plane - 1 + replicas - 1)
    gather.start()

    inputs[2].wait()
    grad_reordered[...] = lax.dot_general(
        place, cotangent[...], CONTRACT_ROWS, preferred_element_type=jnp.float32
    )

    gather.relay()

    for copy in inputs[3:]:
        copy.wait()
    for chunk in range(chunks):
        tile_copy(chunk).wait()

    gather.finish()

    live = tile_count[0, 0]
    first_block = row * row_blocks

    def aggregate(step, acc):
        left, right = [], []
        for sub in range(unroll):
            slot = step * unroll + sub
            col = tile_col[slot]
            position = lax.div(col, row_blocks)
            if half_blocks > 1:
                position = position * half_blocks + lax.rem(col, half_blocks)
            block = jnp.where(slot < live, tile_row[slot] - first_block, row_blocks)
            left.append(tiles[slot])
            right.append(
                jnp.concatenate(
                    [
                        sources[jnp.where(block == which, position, zero_block)]
                        for which in range(row_blocks)
                    ],
                    axis=1,
                )
            )
        return acc + jnp.dot(
            jnp.concatenate(left, axis=1),
            jnp.concatenate(right, axis=0),
            preferred_element_type=jnp.float32,
        )

    acc = lax.fori_loop(
        0, slots // unroll, aggregate, jnp.zeros((tile_size, row_blocks * feat_width), jnp.float32)
    )
    for which in range(row_blocks):
        parts[replica, which] = acc[:, which * feat_width:(which + 1) * feat_width]

    def part_copy(source, target):
        return pltpu.make_async_remote_copy(
            src_ref=parts.at[source],
            dst_ref=parts.at[source],
            send_sem=part_send.at[target],
            recv_sem=part_recv.at[source],
            device_id=(row, target),
            device_id_type=MESH,
        )

    for off in range(1, replicas):
        part_copy(replica, lax.rem(replica + off, replicas)).start()
    for off in range(1, replicas):
        part_copy(lax.rem(replica + replicas - off, replicas), replica).wait_recv()

    total = parts[0]
    for which in range(1, replicas):
        total = total + parts[which]
    hidden = total.reshape(nodes, feat_width).astype(jnp.bfloat16)
    pre_act = jnp.dot(hidden, weight[...], preferred_element_type=jnp.float32) + bias[...]
    sigma = 1.0 / (1.0 + jnp.exp(-pre_act))
    slope = sigma * (1.0 + pre_act * (1.0 - sigma))
    scaled = (grad_reordered[...] * slope).astype(jnp.bfloat16)
    weight_term = lax.dot_general(
        hidden, scaled, CONTRACT_ROWS, preferred_element_type=jnp.float32
    )
    own_term = weight_term[:, :col_width]
    for which in range(1, replicas):
        own_term = jnp.where(
            replica == which, weight_term[:, which * col_width:(which + 1) * col_width], own_term
        )
    bias_term = jnp.sum(scaled.astype(jnp.float32), axis=0, keepdims=True)
    bias_high = bias_term.astype(jnp.bfloat16).astype(jnp.float32)
    bias_rows = [
        part[:, j * col_width:(j + 1) * col_width]
        for part in (bias_high, bias_term - bias_high)
        for j in range(replicas)
    ]
    pad = jnp.zeros((BIAS_ROWS - 2 * replicas, col_width), jnp.float32)
    terms[row, :feat_width] = own_term.astype(jnp.bfloat16)
    terms[row, feat_width:] = jnp.concatenate(bias_rows + [pad], axis=0).astype(jnp.bfloat16)
    reduction.start()

    activated[...] = jnp.dot(
        place, (pre_act * sigma).astype(jnp.bfloat16), preferred_element_type=jnp.float32
    ).astype(jnp.bfloat16)
    act_copy = pltpu.make_async_copy(activated, act_out, act_sem)
    act_copy.start()

    reduction.relay()
    reduction.finish()

    summed = terms[0].astype(jnp.float32)
    for k in range(1, n_rows):
        summed = summed + terms[k].astype(jnp.float32)
    summed = summed * float(nodes * n_rows) ** (-0.5)
    finals[replica] = summed[:feat_width]

    def final_copy(source, target):
        return pltpu.make_async_remote_copy(
            src_ref=finals.at[source],
            dst_ref=finals.at[source],
            send_sem=final_send.at[target],
            recv_sem=final_recv.at[source],
            device_id=(row, target),
            device_id_type=MESH,
        )

    for off in range(1, replicas):
        final_copy(replica, lax.rem(replica + off, replicas)).start()
    for j in range(replicas):
        high, low = feat_width + j, feat_width + replicas + j
        bias_out[:, j * col_width:(j + 1) * col_width] = (
            summed[high:high + 1] + summed[low:low + 1]
        )
    gather.drain()
    reduction.drain()
    for off in range(1, replicas):
        part_copy(replica, lax.rem(replica + off, replicas)).wait_send()
    act_copy.wait()
    for off in range(1, replicas):
        final_copy(lax.rem(replica + replicas - off, replicas), replica).wait_recv()
    for j in range(replicas):
        weight_out[:, j * col_width:(j + 1) * col_width] = finals[j]
    for off in range(1, replicas):
        final_copy(replica, lax.rem(replica + off, replicas)).wait_send()


def publish(act_in, weight_in, bias_in, act_out, weight_out, bias_out, sem):
    copies = [
        pltpu.make_async_copy(source, target, sem.at[k])
        for k, (source, target) in enumerate(
            [(act_in, act_out), (weight_in, weight_out), (bias_in, bias_out)]
        )
    ]
    for copy in copies:
        copy.start()
    for copy in copies:
        copy.wait()


def body(n_rows, replicas, features, node_order, tile_vals, tile_row, tile_col, tile_count, weight, bias, cotangent):
    nodes, feat_width = features.shape
    hid = cotangent.shape[1]
    slots, tile_size, _ = tile_vals.shape
    row_blocks = nodes // tile_size
    half_blocks = row_blocks // replicas
    col_width = hid // replicas
    plane = math.gcd(n_rows, 4)
    depth = n_rows // plane
    chunks = 4
    vmem = pl.BlockSpec(memory_space=pltpu.VMEM)
    dma = pltpu.SemaphoreType.DMA
    activations, weight_grad, bias_grad = pl.pallas_call(
        functools.partial(kernel, n_rows, replicas, plane, chunks, 24),
        out_shape=(
            jax.ShapeDtypeStruct((nodes, hid), jnp.bfloat16),
            jax.ShapeDtypeStruct((feat_width, hid), jnp.float32),
            jax.ShapeDtypeStruct((1, hid), jnp.float32),
        ),
        in_specs=[pl.BlockSpec(memory_space=pltpu.HBM)] * 9,
        out_specs=(pl.BlockSpec(memory_space=pltpu.HBM), vmem, vmem),
        scratch_shapes=[
            pltpu.SMEM(tile_row.shape, jnp.int32),
            pltpu.SMEM(tile_col.shape, jnp.int32),
            pltpu.SMEM((1, 1), jnp.int32),
            pltpu.VMEM((1, nodes), jnp.int32),
            pltpu.VMEM(features.shape, features.dtype),
            pltpu.VMEM(weight.shape, weight.dtype),
            pltpu.VMEM((1, hid), jnp.float32),
            pltpu.VMEM(cotangent.shape, cotangent.dtype),
            pltpu.VMEM((nodes, hid), jnp.bfloat16),
            dma((8,)),
            dma(()),
            pltpu.VMEM((slots, tile_size, tile_size), jnp.bfloat16),
            pltpu.VMEM((n_rows * half_blocks + 1, tile_size, feat_width), jnp.bfloat16),
            pltpu.VMEM((nodes, hid), jnp.float32),
            pltpu.VMEM((replicas, row_blocks, tile_size, feat_width), jnp.float32),
            pltpu.VMEM((n_rows, feat_width + BIAS_ROWS, col_width), jnp.bfloat16),
            pltpu.VMEM((replicas, feat_width, col_width), jnp.float32),
            dma((chunks,)),
            dma((depth,)),
            dma((depth, plane)),
            dma((n_rows,)),
            dma((replicas,)),
            dma((replicas,)),
            dma((depth,)),
            dma((depth, plane)),
            dma((n_rows,)),
            dma((replicas,)),
            dma((replicas,)),
        ],
        compiler_params=pltpu.CompilerParams(
            collective_id=0, has_side_effects=True, vmem_limit_bytes=67043328
        ),
    )(*(
        operand
        for operand in (
            tile_row, tile_col, tile_count.reshape(1, 1), node_order.reshape(1, nodes), features, weight,
            bias.reshape(1, hid), cotangent, tile_vals,
        )
    ))
    activations, weight_grad, bias_grad = pl.pallas_call(
        publish,
        out_shape=tuple(
            jax.ShapeDtypeStruct(part.shape, part.dtype)
            for part in (activations, weight_grad, bias_grad)
        ),
        in_specs=[vmem] * 3,
        out_specs=(pl.BlockSpec(memory_space=pltpu.HBM),) * 3,
        scratch_shapes=[dma((3,))],
    )(activations, weight_grad, bias_grad)
    return activations, weight_grad, bias_grad.reshape(hid)


def solution(mesh):
    return jax.shard_map(
        functools.partial(body, mesh.shape["rows"], mesh.shape["rep"]),
        mesh=mesh,
        in_specs=(
            P("rows", None),
            P("rows"),
            P(("rows", "rep"), None, None),
            P(("rows", "rep")),
            P(("rows", "rep")),
            P(("rows", "rep")),
            P(),
            P(),
            P("rows", None),
        ),
        out_specs=(P("rows", None), P(), P()),
        check_vma=False,
    )
```

time: 50.5 us -> 34.8 us (0.69)
  the two profiles are of different devices: /device:TPU:15 before, /device:TPU:0 now
where the time goes in v2:
time: 34.8 us; the launch traced here: 34.6 us
  Pallas kernels  33.4 us (96%)
  between operations  1.29 us (4%)
    pallas_call x1, Pallas kernels, body(): pl.pallas_call(functools.partial(kernel, n_rows, replicas, plane, chunks,...  31.7 us
    pallas_call x1, Pallas kernels, body(): pl.pallas_call(publish, out_shape=tuple((jax.ShapeDtypeStruct(part.shape,...  1.7 us

profile of v2, /device:TPU:0, one launch (start us, length us, event | category | flops | bytes accessed | tf_op | source)
XLA Modules:
  0.0 34.6 jit_solution(6337158046074842996)
XLA Ops:
  1.3 31.7 %shard_map.112 = (bf16[256,256]{1,0:T(8,128)(2,1)}, f32[128,256]{1,0:T(8,128)}, f32[1,256]{1,0:T(1,128)}) custom-call(s32[192]{0:T(256)} %tile_row_hbm.1, s32[192]{0:T(256)} %tile_col_hbm.1, s32[1,1]{1,0:T(1,128)} %bitcast.4.tile_count_hbm, s32[1,256]{1,0:T(1,128)} %bitcast.5, bf16[256,128]{1,0:T(8,128)(2,1)} %features_hbm.1, bf16[128,256]{1,0:T(8,128)(2,1)} %weight_hbm.1, ...), custom_call_target="tpu_custom_call" | custom-call | tf_op jit(solution)/shard_map/pallas_call | solution.py:320
  32.9 1.7 %shard_map.113 = (bf16[256,256]{1,0:T(8,128)(2,1)}, f32[128,256]{1,0:T(8,128)}, f32[1,256]{1,0:T(1,128)}) custom-call(bf16[256,256]{1,0:T(8,128)(2,1)} %get-tuple-element.9.act_in, f32[128,256]{1,0:T(8,128)} %get-tuple-element.10.weight_in, f32[1,256]{1,0:T(1,128)} %get-tuple-element.11.bias_in), custom_call_target="tpu_custom_call" | custom-call | tf_op jit(solution)/shard_map/pallas_call | solution.py:369

commit v3 on v2

--- a/solution.py
+++ b/solution.py
@@ -19,9 +19,9 @@
     cotangent_hbm, tiles_hbm,
     act_out, weight_out, bias_out,
     tile_row, tile_col, tile_count, order, features, weight, bias, cotangent, activated, input_sem,
-    act_sem, tiles, sources, grad_reordered, parts, terms, finals,
+    act_sem, tiles, sources, grad_reordered, parts, terms, sums, finals,
     tile_sem, gather_column, gather_plane, gather_recv, part_send, part_recv,
-    term_column, term_plane, term_recv, final_send, final_recv,
+    term_send, term_recv, sum_send, sum_recv, final_send, final_recv,
 ):
     row = lax.axis_index("rows")
     replica = lax.axis_index("rep")
@@ -138,7 +138,6 @@
         return sources.at[pl.ds(block * half_blocks, half_blocks)]
 
     gather = Spread(source_view, gather_column, gather_plane, gather_recv)
-    reduction = Spread(lambda block: terms.at[block], term_column, term_plane, term_recv)
 
     inputs[0].wait()
     inputs[1].wait()
@@ -236,16 +235,50 @@
             replica == which, weight_term[:, which * col_width:(which + 1) * col_width], own_term
         )
     bias_term = jnp.sum(scaled.astype(jnp.float32), axis=0, keepdims=True)
-    bias_high = bias_term.astype(jnp.bfloat16).astype(jnp.float32)
-    bias_rows = [
-        part[:, j * col_width:(j + 1) * col_width]
-        for part in (bias_high, bias_term - bias_high)
-        for j in range(replicas)
-    ]
-    pad = jnp.zeros((BIAS_ROWS - 2 * replicas, col_width), jnp.float32)
-    terms[row, :feat_width] = own_term.astype(jnp.bfloat16)
-    terms[row, feat_width:] = jnp.concatenate(bias_rows + [pad], axis=0).astype(jnp.bfloat16)
-    reduction.start()
+    bias_term = jnp.concatenate(
+        [bias_term[:, j * col_width:(j + 1) * col_width] for j in range(replicas)], axis=0
+    )
+
+    def pack(target, term, bias_part):
+        high = bias_part.astype(jnp.bfloat16).astype(jnp.float32)
+        pad = jnp.zeros((BIAS_ROWS - 2 * replicas, col_width), jnp.float32)
+        target[:feat_width] = term.astype(jnp.bfloat16)
+        target[feat_width:] = jnp.concatenate([high, bias_part - high, pad], axis=0).astype(
+            jnp.bfloat16
+        )
+
+    def unpack(held):
+        summed = held[0].astype(jnp.float32)
+        for k in range(1, held.shape[0]):
+            summed = summed + held[k].astype(jnp.float32)
+        low = feat_width + replicas
+        return summed[:feat_width], summed[feat_width:low] + summed[low:low + replicas]
+
+    def term_copy(source, off):
+        return pltpu.make_async_remote_copy(
+            src_ref=terms.at[source],
+            dst_ref=terms.at[source],
+            send_sem=term_send.at[off],
+            recv_sem=term_recv.at[source],
+            device_id=(column_peer(off), replica),
+            device_id_type=MESH,
+        )
+
+    def sum_copy(source, off):
+        return pltpu.make_async_remote_copy(
+            src_ref=sums.at[source],
+            dst_ref=sums.at[source],
+            send_sem=sum_send.at[off],
+            recv_sem=sum_recv.at[source],
+            device_id=(plane_peer(off), replica),
+            device_id_type=MESH,
+        )
+
+    pack(terms.at[layer], own_term, bias_term)
+
+    @pl.loop(1, depth)
+    def _(off):
+        term_copy(layer, depth - off).start()
 
     activated[...] = jnp.dot(
         place, (pre_act * sigma).astype(jnp.bfloat16), preferred_element_type=jnp.float32
@@ -253,14 +286,20 @@
     act_copy = pltpu.make_async_copy(activated, act_out, act_sem)
     act_copy.start()
 
-    reduction.relay()
-    reduction.finish()
-
-    summed = terms[0].astype(jnp.float32)
-    for k in range(1, n_rows):
-        summed = summed + terms[k].astype(jnp.float32)
-    summed = summed * float(nodes * n_rows) ** (-0.5)
-    finals[replica] = summed[:feat_width]
+    @pl.loop(1, depth)
+    def _(off):
+        term_copy(lax.rem(layer + toward * off + depth, depth), off).wait_recv()
+
+    pack(sums.at[spot], *unpack(terms))
+    for off in range(1, plane):
+        sum_copy(spot, off).start()
+    gather.drain()
+    for off in range(1, plane):
+        sum_copy(lax.rem(spot + off, plane), off).wait_recv()
+
+    weight_sum, bias_sum = unpack(sums)
+    grad_scale = float(nodes * n_rows) ** (-0.5)
+    finals[replica] = weight_sum * grad_scale
 
     def final_copy(source, target):
         return pltpu.make_async_remote_copy(
@@ -275,12 +314,14 @@
     for off in range(1, replicas):
         final_copy(replica, lax.rem(replica + off, replicas)).start()
     for j in range(replicas):
-        high, low = feat_width + j, feat_width + replicas + j
-        bias_out[:, j * col_width:(j + 1) * col_width] = (
-            summed[high:high + 1] + summed[low:low + 1]
-        )
-    gather.drain()
-    reduction.drain()
+        bias_out[:, j * col_width:(j + 1) * col_width] = bias_sum[j:j + 1] * grad_scale
+
+    @pl.loop(1, depth)
+    def _(off):
+        term_copy(layer, off).wait_send()
+
+    for off in range(1, plane):
+        sum_copy(spot, off).wait_send()
     for off in range(1, replicas):
         part_copy(replica, lax.rem(replica + off, replicas)).wait_send()
     act_copy.wait()
@@ -317,6 +358,7 @@
     chunks = 4
     vmem = pl.BlockSpec(memory_space=pltpu.VMEM)
     dma = pltpu.SemaphoreType.DMA
+    tile_total = tile_count.reshape(1, 1)
     activations, weight_grad, bias_grad = pl.pallas_call(
         functools.partial(kernel, n_rows, replicas, plane, chunks, 24),
         out_shape=(
@@ -342,7 +384,8 @@
             pltpu.VMEM((n_rows * half_blocks + 1, tile_size, feat_width), jnp.bfloat16),
             pltpu.VMEM((nodes, hid), jnp.float32),
             pltpu.VMEM((replicas, row_blocks, tile_size, feat_width), jnp.float32),
-            pltpu.VMEM((n_rows, feat_width + BIAS_ROWS, col_width), jnp.bfloat16),
+            pltpu.VMEM((depth, feat_width + BIAS_ROWS, col_width), jnp.bfloat16),
+            pltpu.VMEM((plane, feat_width + BIAS_ROWS, col_width), jnp.bfloat16),
             pltpu.VMEM((replicas, feat_width, col_width), jnp.float32),
             dma((chunks,)),
             dma((depth,)),
@@ -351,18 +394,19 @@
             dma((replicas,)),
             dma((replicas,)),
             dma((depth,)),
-            dma((depth, plane)),
-            dma((n_rows,)),
+            dma((depth,)),
+            dma((plane,)),
+            dma((plane,)),
             dma((replicas,)),
             dma((replicas,)),
         ],
         compiler_params=pltpu.CompilerParams(
-            collective_id=0, has_side_effects=True, vmem_limit_bytes=67043328
+            collective_id=0, has_side_effects=True, vmem_limit_bytes=48 * 1024 * 1024
         ),
     )(*(
-        operand
+        operand if operand is tile_total else pltpu.with_memory_space_constraint(operand, pltpu.HBM)
         for operand in (
-            tile_row, tile_col, tile_count.reshape(1, 1), node_order.reshape(1, nodes), features, weight,
+            tile_row, tile_col, tile_total, node_order.reshape(1, nodes), features, weight,
             bias.reshape(1, hid), cotangent, tile_vals,
         )
     ))
@@ -375,6 +419,7 @@
         in_specs=[vmem] * 3,
         out_specs=(pl.BlockSpec(memory_space=pltpu.HBM),) * 3,
         scratch_shapes=[dma((3,))],
+        compiler_params=pltpu.CompilerParams(vmem_limit_bytes=1024 * 1024),
     )(activations, weight_grad, bias_grad)
     return activations, weight_grad, bias_grad.reshape(hid)
 

time: 34.8 us -> 30.4 us (0.87)
  Pallas kernels: 33.4 us -> 28.9 us
    pallas_call x1, Pallas kernels: 31.7 us -> 28.2 us  [body(): pl.pallas_call(functools.partial(kernel, n_rows, replicas, plane, chunks,...]
    pallas_call x1, Pallas kernels: 1.7 us -> 0.73 us  [body(): pl.pallas_call(publish, out_shape=tuple((jax.ShapeDtypeStruct(part.shape,...]
where the time goes in v3:
time: 30.4 us; the launch traced here: 30.2 us
  Pallas kernels  28.9 us (95%)
  between operations  1.29 us (4%)
    pallas_call x1, Pallas kernels, body(): pl.pallas_call(functools.partial(kernel, n_rows, replicas, plane, chunks,...  28.2 us
    pallas_call x1, Pallas kernels, body(): pl.pallas_call(publish, out_shape=tuple((jax.ShapeDtypeStruct(part.shape,...  0.73 us

profile of v3, /device:TPU:0, one launch (start us, length us, event | category | flops | bytes accessed | tf_op | source)
XLA Modules:
  0.0 30.2 jit_solution(4155974387651821629)
XLA Ops:
  1.3 28.2 %shard_map.112 = (bf16[256,256]{1,0:T(8,128)(2,1)S(1)}, f32[128,256]{1,0:T(8,128)S(1)}, f32[1,256]{1,0:T(1,128)S(1)}) custom-call(s32[192]{0:T(256)} %tile_row_hbm.1, s32[192]{0:T(256)} %tile_col_hbm.1, s32[1,1]{1,0:T(1,128)} %bitcast.4.tile_count_hbm, s32[1,256]{1,0:T(1,128)} %bitcast.5, bf16[256,128]{1,0:T(8,128)(2,1)} %features_hbm.1, ...), custom_call_target="tpu_custom_call" | custom-call | tf_op jit(solution)/shard_map/pallas_call | solution.py:362
  29.5 0.7 %shard_map.113 = (bf16[256,256]{1,0:T(8,128)(2,1)}, f32[128,256]{1,0:T(8,128)}, f32[1,256]{1,0:T(1,128)}) custom-call(bf16[256,256]{1,0:T(8,128)(2,1)S(1)} %get-tuple-element.9.act_in, f32[128,256]{1,0:T(8,128)S(1)} %get-tuple-element.10.weight_in, f32[1,256]{1,0:T(1,128)S(1)} %get-tuple-element.11.bias_in), custom_call_target="tpu_custom_call" | custom-call | tf_op jit(solution)/shard_map/pallas_call | solution.py:413

commit v4 on v3

--- a/solution.py
+++ b/solution.py
@@ -360,7 +360,7 @@
     dma = pltpu.SemaphoreType.DMA
     tile_total = tile_count.reshape(1, 1)
     activations, weight_grad, bias_grad = pl.pallas_call(
-        functools.partial(kernel, n_rows, replicas, plane, chunks, 24),
+        functools.partial(kernel, n_rows, replicas, plane, chunks, 48),
         out_shape=(
             jax.ShapeDtypeStruct((nodes, hid), jnp.bfloat16),
             jax.ShapeDtypeStruct((feat_width, hid), jnp.float32),

time: 30.4 us -> 29.6 us (0.974)
  Pallas kernels: 28.9 us -> 28.2 us
    pallas_call x1, Pallas kernels: 28.2 us -> 27.4 us  [body(): pl.pallas_call(functools.partial(kernel, n_rows, replicas, plane, chunks,...]
where the time goes in v4:
time: 29.6 us; the launch traced here: 29.4 us
  Pallas kernels  28.2 us (95%)
  between operations  1.29 us (4%)
    pallas_call x1, Pallas kernels, body(): pl.pallas_call(functools.partial(kernel, n_rows, replicas, plane, chunks,...  27.4 us
    pallas_call x1, Pallas kernels, body(): pl.pallas_call(publish, out_shape=tuple((jax.ShapeDtypeStruct(part.shape,...  0.73 us

profile of v4, /device:TPU:0, one launch (start us, length us, event | category | flops | bytes accessed | tf_op | source)
XLA Modules:
  0.0 29.4 jit_solution(1651635607541112991)
XLA Ops:
  1.3 27.4 %shard_map.112 = (bf16[256,256]{1,0:T(8,128)(2,1)S(1)}, f32[128,256]{1,0:T(8,128)S(1)}, f32[1,256]{1,0:T(1,128)S(1)}) custom-call(s32[192]{0:T(256)} %tile_row_hbm.1, s32[192]{0:T(256)} %tile_col_hbm.1, s32[1,1]{1,0:T(1,128)} %bitcast.4.tile_count_hbm, s32[1,256]{1,0:T(1,128)} %bitcast.5, bf16[256,128]{1,0:T(8,128)(2,1)} %features_hbm.1, ...), custom_call_target="tpu_custom_call" | custom-call | tf_op jit(solution)/shard_map/pallas_call | solution.py:362
  28.7 0.7 %shard_map.113 = (bf16[256,256]{1,0:T(8,128)(2,1)}, f32[128,256]{1,0:T(8,128)}, f32[1,256]{1,0:T(1,128)}) custom-call(bf16[256,256]{1,0:T(8,128)(2,1)S(1)} %get-tuple-element.9.act_in, f32[128,256]{1,0:T(8,128)S(1)} %get-tuple-element.10.weight_in, f32[1,256]{1,0:T(1,128)S(1)} %get-tuple-element.11.bias_in), custom_call_target="tpu_custom_call" | custom-call | tf_op jit(solution)/shard_map/pallas_call | solution.py:413
